TPU v7x, 32 devices: a whole 2x2x4 slice. The times are simulated.
32 devices in a mesh: px: 8 (over z, y), py: 4 (over x, core).
Axes of the slice: x: 2, y: 2, z: 4, core: 2. Of those that a mesh axis runs over, the one named last changes fastest.
Arguments:
- spectrum: float32 [2, 1536, 24576], P(None, 'px', 'py'), may hold values from -6 to 6
- concentration: float32 [3072, 24576], P('px', 'py'), may hold values from -6 to 6
- factor_y: float32 [1536, 128], P('py'), may hold values from -0.15625 to 0.15625
- factor_x: float32 [3072, 256], P('px'), may hold values from -0.109375 to 0.109375
Outputs:
- y_compressed: float32 [16, 3072, 128], P('py', 'px')
- core_tensor: float32 [16, 256, 128], P('py', 'px')
All inputs are finite; a program needn't handle non-finite values.
Results may differ from a plain program's by a relative error of at most 0.000076.
Values sent between devices are 32-bit elements; how exact they have to be, the bound alone decides.
No kernel may reach another device: no remote copies, remote signals or barrier semaphores. Data moves between devices by JAX's collectives and lax.ppermute only.
A program may use at most 128 MiB of HBM per device.

v0:
```python
import math
import jax
import jax.numpy as jnp
from jax import lax
from jax.sharding import PartitionSpec as P

NX = 3072
NZ = 16
KX = 1536


def synth_table(first_x, block_width):
    wave = lax.broadcasted_iota(jnp.int32, (KX, block_width), 0)
    column = first_x + lax.broadcasted_iota(jnp.int32, (KX, block_width), 1)
    phase = wave * column % NX
    angle = phase.astype(jnp.float32) * (2.0 * math.pi / NX)
    weight = jnp.where(wave == 0, 1.0, 2.0) / math.sqrt(KX)
    return jnp.concatenate([weight * jnp.cos(angle), -weight * jnp.sin(angle)], axis=0)


def body(spectrum, concentration, factor_y, factor_x):
    x_local = concentration.shape[0]
    line_total = concentration.shape[1]
    y_local = line_total // NZ
    pencil_modes = lax.all_to_all(spectrum, "px", split_axis=2, concat_axis=1, tiled=True)
    line_count = pencil_modes.shape[2]
    stacked_modes = pencil_modes.reshape(2 * KX, line_count)
    block_width = 512
    block_total = NX // block_width

    def fill_block(block_index, velocity):
        first_x = block_index * block_width
        rows = lax.dot_general(
            synth_table(first_x, block_width),
            stacked_modes,
            (((0,), (0,)), ((), ())),
            precision=lax.Precision.HIGHEST,
            preferred_element_type=jnp.float32,
        )
        return lax.dynamic_update_slice_in_dim(velocity, rows, first_x, 0)

    velocity = lax.fori_loop(0, block_total, fill_block, jnp.zeros((NX, line_count), jnp.float32))
    returned = lax.all_to_all(velocity, "px", split_axis=0, concat_axis=1, tiled=True)
    flux_tile = returned * concentration
    flux_cube = flux_tile.reshape(x_local, y_local, NZ)
    rows = flux_cube
    y_compressed = lax.psum_scatter(
        jnp.einsum("xyz,yr->zxr", rows, factor_y, precision=lax.Precision.HIGHEST),
        "py",
        scatter_dimension=0,
        tiled=True,
    )
    core_terms = jnp.einsum("xs,zxr->zsr", factor_x, y_compressed, precision=lax.Precision.HIGHEST)
    core_tensor = lax.psum_scatter(core_terms, "px", scatter_dimension=1, tiled=True)
    return (y_compressed, core_tensor)


def solution(mesh):
    placed = (P(None, "px", "py"), P("px", "py"), P("py", None), P("px", None))
    return jax.shard_map(
        body,
        mesh=mesh,
        in_specs=placed,
        out_specs=(P("py", "px", None), P("py", "px", None)),
        check_vma=False,
    )
```

profile of v0, /device:TPU:0, one launch (start us, length us, event | category | flops | bytes accessed | tf_op | source)
XLA Modules:
  0.0 983.5 jit_solution(7462423224211802599)
XLA Ops:
  7.2 18.4 %copy.17 = f32[2,192,6144]{1,0,2:T(2,128)} copy(f32[2,192,6144]{2,1,0:T(8,128)} %param.6) | data formatting | bytes 18874368 | tf_op args[0]
  25.6 7.3 all-to-all-start
  32.9 273.1 %all-to-all-done = f32[2,192,6144]{1,0,2:T(2,128)} async-done(((f32[2,192,6144]{1,0,2:T(2,128)}), f32[2,192,6144]{1,0,2:T(2,128)}, u32[]{:S(2)}, u32[]{:S(2)}) %all-to-all-start) | async-done | bytes 9437216 | tf_op jit(solution)/shard_map/all_to_all | solution.py:25
  306.0 18.3 %copy.18 = f32[2,8,192,768]{3,2,1,0:T(8,128)} copy(f32[2,8,192,768]{2,0,3,1:T(2,128)} %bitcast.1) | data formatting | bytes 18874368 | tf_op jit(solution)/shard_map/all_to_all | solution.py:25
  328.5 281.5 %while.15 = (s32[]{:T(128)}, f32[3072,768]{1,0:T(8,128)}, f32[3072,768]{1,0:T(8,128)}, s32[]{:T(128)}, s32[]{:T(128)}, /*index=5*/s32[]{:T(128)}, s32[]{:T(128)}) while((s32[]{:T(128)}, f32[3072,768]{1,0:T(8,128)}, f32[3072,768]{1,0:T(8,128)}, s32[]{:T(128)}, s32[]{:T(128)}, /*index=5*/s32[]{:T(128)}, s32[]{:T(128)}) %tuple.56), condition=%wide.region_1.2_spmd, body=%wide.region_0.1_spmd.sunk | while | flops 14505745408 | bytes 23621764 | solution.py:42
  328.5 13.5 %cosine_multiply_fusion.2 = (f32[1536,512]{1,0:T(8,128)S(1)}, f32[1536,512]{1,0:T(8,128)S(1)}) fusion(s32[512]{0:T(512)S(1)} %iota_add_fusion.2, f32[1536]{0:T(1024)S(1)} %get-tuple-element.131, f32[1536]{0:T(1024)S(1)} %get-tuple-element.132), kind=kLoop, calls=%fused_computation.8.clone.1 | loop fusion | flops 8650752 | bytes 6305792 | tf_op jit(solution)/shard_map/while/body/eval_jaxpr/mul | solution.py:18
  342.1 33.4 %fusion.28 = f32[3072,768]{1,0:T(8,128)} fusion(f32[3072,768]{1,0:T(8,128)} %get-tuple-element.143, s32[]{:T(128)S(6)} %select_n.61, f32[3072,768]{1,0:T(8,128)} %get-tuple-element.151, f32[1536,512]{1,0:T(8,128)S(1)} %get-tuple-element.133, f32[1536,512]{1,0:T(8,128)S(1)} %get-tuple-element.134), kind=kOutput, calls=%fused_computation.13.clone.1 | convolution fusion | flops 14497087488 | bytes 17301508 | tf_op jit(solution)/shard_map/while/body/eval_jaxpr/dot_general | solution.py:33
  375.4 13.5 %cosine_multiply_fusion.2 = (f32[1536,512]{1,0:T(8,128)S(1)}, f32[1536,512]{1,0:T(8,128)S(1)}) fusion(s32[512]{0:T(512)S(1)} %iota_add_fusion.2, f32[1536]{0:T(1024)S(1)} %get-tuple-element.131, f32[1536]{0:T(1024)S(1)} %get-tuple-element.132), kind=kLoop, calls=%fused_computation.8.clone.1 | loop fusion | flops 8650752 | bytes 6305792 | tf_op jit(solution)/shard_map/while/body/eval_jaxpr/mul | solution.py:18
  388.9 33.4 %fusion.28 = f32[3072,768]{1,0:T(8,128)} fusion(f32[3072,768]{1,0:T(8,128)} %get-tuple-element.143, s32[]{:T(128)S(6)} %select_n.61, f32[3072,768]{1,0:T(8,128)} %get-tuple-element.151, f32[1536,512]{1,0:T(8,128)S(1)} %get-tuple-element.133, f32[1536,512]{1,0:T(8,128)S(1)} %get-tuple-element.134), kind=kOutput, calls=%fused_computation.13.clone.1 | convolution fusion | flops 14497087488 | bytes 17301508 | tf_op jit(solution)/shard_map/while/body/eval_jaxpr/dot_general | solution.py:33
  422.4 13.5 %cosine_multiply_fusion.2 = (f32[1536,512]{1,0:T(8,128)S(1)}, f32[1536,512]{1,0:T(8,128)S(1)}) fusion(s32[512]{0:T(512)S(1)} %iota_add_fusion.2, f32[1536]{0:T(1024)S(1)} %get-tuple-element.131, f32[1536]{0:T(1024)S(1)} %get-tuple-element.132), kind=kLoop, calls=%fused_computation.8.clone.1 | loop fusion | flops 8650752 | bytes 6305792 | tf_op jit(solution)/shard_map/while/body/eval_jaxpr/mul | solution.py:18
  435.9 33.4 %fusion.28 = f32[3072,768]{1,0:T(8,128)} fusion(f32[3072,768]{1,0:T(8,128)} %get-tuple-element.143, s32[]{:T(128)S(6)} %select_n.61, f32[3072,768]{1,0:T(8,128)} %get-tuple-element.151, f32[1536,512]{1,0:T(8,128)S(1)} %get-tuple-element.133, f32[1536,512]{1,0:T(8,128)S(1)} %get-tuple-element.134), kind=kOutput, calls=%fused_computation.13.clone.1 | convolution fusion | flops 14497087488 | bytes 17301508 | tf_op jit(solution)/shard_map/while/body/eval_jaxpr/dot_general | solution.py:33
  469.3 13.5 %cosine_multiply_fusion.2 = (f32[1536,512]{1,0:T(8,128)S(1)}, f32[1536,512]{1,0:T(8,128)S(1)}) fusion(s32[512]{0:T(512)S(1)} %iota_add_fusion.2, f32[1536]{0:T(1024)S(1)} %get-tuple-element.131, f32[1536]{0:T(1024)S(1)} %get-tuple-element.132), kind=kLoop, calls=%fused_computation.8.clone.1 | loop fusion | flops 8650752 | bytes 6305792 | tf_op jit(solution)/shard_map/while/body/eval_jaxpr/mul | solution.py:18
  482.8 33.4 %fusion.28 = f32[3072,768]{1,0:T(8,128)} fusion(f32[3072,768]{1,0:T(8,128)} %get-tuple-element.143, s32[]{:T(128)S(6)} %select_n.61, f32[3072,768]{1,0:T(8,128)} %get-tuple-element.151, f32[1536,512]{1,0:T(8,128)S(1)} %get-tuple-element.133, f32[1536,512]{1,0:T(8,128)S(1)} %get-tuple-element.134), kind=kOutput, calls=%fused_computation.13.clone.1 | convolution fusion | flops 14497087488 | bytes 17301508 | tf_op jit(solution)/shard_map/while/body/eval_jaxpr/dot_general | solution.py:33
  516.2 13.5 %cosine_multiply_fusion.2 = (f32[1536,512]{1,0:T(8,128)S(1)}, f32[1536,512]{1,0:T(8,128)S(1)}) fusion(s32[512]{0:T(512)S(1)} %iota_add_fusion.2, f32[1536]{0:T(1024)S(1)} %get-tuple-element.131, f32[1536]{0:T(1024)S(1)} %get-tuple-element.132), kind=kLoop, calls=%fused_computation.8.clone.1 | loop fusion | flops 8650752 | bytes 6305792 | tf_op jit(solution)/shard_map/while/body/eval_jaxpr/mul | solution.py:18
  529.7 33.4 %fusion.28 = f32[3072,768]{1,0:T(8,128)} fusion(f32[3072,768]{1,0:T(8,128)} %get-tuple-element.143, s32[]{:T(128)S(6)} %select_n.61, f32[3072,768]{1,0:T(8,128)} %get-tuple-element.151, f32[1536,512]{1,0:T(8,128)S(1)} %get-tuple-element.133, f32[1536,512]{1,0:T(8,128)S(1)} %get-tuple-element.134), kind=kOutput, calls=%fused_computation.13.clone.1 | convolution fusion | flops 14497087488 | bytes 17301508 | tf_op jit(solution)/shard_map/while/body/eval_jaxpr/dot_general | solution.py:33
  563.1 13.5 %cosine_multiply_fusion.2 = (f32[1536,512]{1,0:T(8,128)S(1)}, f32[1536,512]{1,0:T(8,128)S(1)}) fusion(s32[512]{0:T(512)S(1)} %iota_add_fusion.2, f32[1536]{0:T(1024)S(1)} %get-tuple-element.131, f32[1536]{0:T(1024)S(1)} %get-tuple-element.132), kind=kLoop, calls=%fused_computation.8.clone.1 | loop fusion | flops 8650752 | bytes 6305792 | tf_op jit(solution)/shard_map/while/body/eval_jaxpr/mul | solution.py:18
  576.6 33.4 %fusion.28 = f32[3072,768]{1,0:T(8,128)} fusion(f32[3072,768]{1,0:T(8,128)} %get-tuple-element.143, s32[]{:T(128)S(6)} %select_n.61, f32[3072,768]{1,0:T(8,128)} %get-tuple-element.151, f32[1536,512]{1,0:T(8,128)S(1)} %get-tuple-element.133, f32[1536,512]{1,0:T(8,128)S(1)} %get-tuple-element.134), kind=kOutput, calls=%fused_computation.13.clone.1 | convolution fusion | flops 14497087488 | bytes 17301508 | tf_op jit(solution)/shard_map/while/body/eval_jaxpr/dot_general | solution.py:33
  610.1 9.5 copy.19
  624.7 9.6 copy.20
  634.4 195.0 %all-to-all-done.1 = f32[8,384,768]{1,2,0:T(8,128)} async-done(((f32[8,384,768]{1,2,0:T(8,128)}), f32[8,384,768]{1,2,0:T(8,128)}, u32[]{:S(2)}, u32[]{:S(2)}) %all-to-all-start.1) | async-done | bytes 9437216 | tf_op jit(solution)/shard_map/all_to_all | solution.py:43
  829.4 11.2 %bitcast_multiply_fusion = f32[384,6144]{0,1:T(8,128)} fusion(f32[384,6144]{0,1:T(8,128)} %copy.20, f32[8,384,768]{1,2,0:T(8,128)} %all-to-all-done.1), kind=kLoop, calls=%fused_computation.19 | loop fusion | flops 2359296 | bytes 28311552 | tf_op jit(solution)/shard_map/mul | solution.py:44
  840.6 21.0 %fusion.16 = f32[16,384,128]{2,1,0:T(8,128)} fusion(f32[384,384,16]{0,2,1:T(8,128)} %bitcast.26, f32[384,128]{1,0:T(8,128)S(1)} %copy-done.1), kind=kOutput, calls=%fused_computation.22 | convolution fusion | flops 3623878656 | bytes 12779520 | tf_op jit(solution)/shard_map/xyz,yr->zxr/dot_general | solution.py:48
  861.7 37.0 %reduce-scatter.2.cloned.1.call-done = f32[4,384,128]{2,1,0:T(8,128)} async-done(((f32[16,384,128]{2,1,0:T(8,128)}), f32[4,384,128]{2,1,0:T(8,128)}) %reduce-scatter.2.cloned.1.call-update) | async-done | bytes 786448 | tf_op jit(solution)/shard_map/reduce_scatter | solution.py:47
  903.6 71.6 %all-reduce.3.cloned.1.call-done = f32[4,256,128]{2,0,1:T(4,128)} async-done(((f32[4,256,128]{2,0,1:T(4,128)}), f32[4,256,128]{2,0,1:T(4,128)}) %all-reduce.3.cloned.1.call-update) | async-done | bytes 524304
  (29 shorter events, 15.1 us)
Async XLA Ops:
  7.2 891.6 %copy-start = (f32[384,256]{1,0:T(8,128)S(1)}, f32[384,256]{1,0:T(8,128)}, u32[]{:S(2)}) copy-start(f32[384,256]{1,0:T(8,128)} %param.9) | copy-start | bytes 1179652
  25.6 280.4 %all-to-all-start = ((f32[2,192,6144]{1,0,2:T(2,128)}), f32[2,192,6144]{1,0,2:T(2,128)}, u32[]{:S(2)}, u32[]{:S(2)}) async-start(f32[2,192,6144]{1,0,2:T(2,128)} %copy.17), calls=%async_computation | async-start | bytes 25165824 | tf_op jit(solution)/shard_map/all_to_all | solution.py:25
  619.6 209.8 %all-to-all-start.1 = ((f32[8,384,768]{1,2,0:T(8,128)}), f32[8,384,768]{1,2,0:T(8,128)}, u32[]{:S(2)}, u32[]{:S(2)}) async-start(f32[8,384,768]{1,2,0:T(8,128)} %copy.19), calls=%async_computation.1 | async-start | bytes 18874368 | tf_op jit(solution)/shard_map/all_to_all | solution.py:43
  624.7 274.1 %reduce-scatter.2.cloned.1.call-start = ((), (), s32[]{:S(2)}) async-start(), calls=%async_computation.3 | async-start | bytes 3932160 | tf_op jit(solution)/shard_map/reduce_scatter | solution.py:47
  634.4 206.3 %copy-start.1 = (f32[384,128]{1,0:T(8,128)S(1)}, f32[384,128]{1,0:T(8,128)}, u32[]{:S(2)}) copy-start(f32[384,128]{1,0:T(8,128)} %param.8) | copy-start | bytes 589828
  861.6 40.7 %copy-start.2 = (u32[32]{0:T(128)S(1)}, u32[32]{0:T(128)}, u32[]{:S(2)}) copy-start(u32[32]{0:T(128)} %constant.99) | copy-start | bytes 388
  861.7 113.6 %all-reduce.3.cloned.1.call-start = ((), (), s32[]{:S(2)}) async-start(), calls=%async_computation.4 | async-start | bytes 1048576
Sparse Core Ops, SparseCore 0:
  861.8 36.9 reduce-scatter.1
  902.5 72.7 all-reduce.2
where the time goes:
time: 985 us; the launch traced here: 984 us
  waiting for transfers between devices  577 us (59%)
  matrix products  224 us (23%)
  other arithmetic  92.3 us (9%)
  local copies, waits for them, and re-layouts  63.2 us (6%)
  between operations  14.7 us (1%)
  starting transfers between devices  12.4 us (1%)
    all_to_all x1, waiting for transfers between devices, body(): lax.all_to_all(spectrum, 'px', split_axis=2, concat_axis=1, tiled=True)  273 us
    dot_general x6, matrix products, fill_block(): lax.dot_general(synth_table(first_x, block_width), stacked_modes, (((0,),...  200 us
    all_to_all x1, waiting for transfers between devices, body(): lax.all_to_all(velocity, 'px', split_axis=0, concat_axis=1, tiled=True)  195 us
    mul x6, other arithmetic, synth_table(): weight * jnp.cos(angle)  81 us
    unnamed x3, waiting for transfers between devices  71.7 us
    reduce_scatter x1, waiting for transfers between devices, body(): lax.psum_scatter(jnp.einsum('xyz,yr->zxr', rows, factor_y, precision=lax....  37 us
    unnamed x11, local copies, waits for them, and re-layouts  30.1 us
    dot_general x1, matrix products, body(): jnp.einsum('xyz,yr->zxr', rows, factor_y, precision=lax.Precision.HIGHEST)  21 us
  transfers between devices with their start and end apart: 4, of which 4 were waited for; matrix products, arithmetic and copies ran while one was open for 1% of the time, Pallas kernels for 0%

commit v1 on v0

--- a/solution.py
+++ b/solution.py
@@ -22,7 +22,10 @@
     x_local = concentration.shape[0]
     line_total = concentration.shape[1]
     y_local = line_total // NZ
-    pencil_modes = lax.all_to_all(spectrum, "px", split_axis=2, concat_axis=1, tiled=True)
+    pencil_modes = jnp.concatenate(
+        lax.all_to_all(jnp.stack(jnp.split(spectrum, lax.axis_size("px"), axis=2)), "px", 0, 0),
+        axis=1,
+    )
     line_count = pencil_modes.shape[2]
     stacked_modes = pencil_modes.reshape(2 * KX, line_count)
     block_width = 512

time: 985 us -> 908 us (0.922)
  waiting for transfers between devices: 577 us -> 509 us
    all_to_all x1, waiting for transfers between devices: 273 us -> 206 us  [body(): lax.all_to_all(jnp.stack(jnp.split(spectrum, lax.axis_size('px'), axis=2)...]
    all_to_all x1 -> x0, local copies, waits for them, and re-layouts: 18.3 us -> none  [body(): lax.all_to_all(spectrum, 'px', split_axis=2, concat_axis=1, tiled=True)]
    unnamed x11 -> x17, local copies, waits for them, and re-layouts: 30.1 us -> 28.5 us
where the time goes in v1:
time: 908 us; the launch traced here: 907 us
  waiting for transfers between devices  509 us (56%)
  matrix products  224 us (25%)
  other arithmetic  92.3 us (10%)
  local copies, waits for them, and re-layouts  53.9 us (6%)
  between operations  14.7 us (2%)
  starting transfers between devices  12.4 us (1%)
    all_to_all x1, waiting for transfers between devices, body(): lax.all_to_all(jnp.stack(jnp.split(spectrum, lax.axis_size('px'), axis=2)...  206 us
    dot_general x6, matrix products, fill_block(): lax.dot_general(synth_table(first_x, block_width), stacked_modes, (((0,),...  200 us
    all_to_all x1, waiting for transfers between devices, body(): lax.all_to_all(velocity, 'px', split_axis=0, concat_axis=1, tiled=True)  195 us
    mul x6, other arithmetic, synth_table(): weight * jnp.cos(angle)  81 us
    unnamed x3, waiting for transfers between devices  71.7 us
    reduce_scatter x1, waiting for transfers between devices, body(): lax.psum_scatter(jnp.einsum('xyz,yr->zxr', rows, factor_y, precision=lax....  37 us
    unnamed x17, local copies, waits for them, and re-layouts  28.5 us
    dot_general x1, matrix products, body(): jnp.einsum('xyz,yr->zxr', rows, factor_y, precision=lax.Precision.HIGHEST)  21 us
  transfers between devices with their start and end apart: 4, of which 4 were waited for; matrix products, arithmetic and copies ran while one was open for 1% of the time, Pallas kernels for 0%

profile of v1, /device:TPU:0, one launch (start us, length us, event | category | flops | bytes accessed | tf_op | source)
XLA Modules:
  0.0 906.9 jit_solution(5710014350999524674)
XLA Ops:
  26.4 7.3 all-to-all-start
  33.7 205.6 %all-to-all-done = f32[8,2,192,768]{3,2,1,0:T(8,128)} async-done(((f32[8,2,192,768]{3,2,1,0:T(8,128)}), f32[8,2,192,768]{3,2,1,0:T(8,128)}, u32[]{:S(2)}, u32[]{:S(2)}) %all-to-all-start) | async-done | bytes 9437216 | tf_op jit(solution)/shard_map/all_to_all | solution.py:26
  239.3 8.2 copy.17
  251.8 281.6 %while.15 = (s32[]{:T(128)}, f32[3072,768]{1,0:T(8,128)}, f32[3072,768]{1,0:T(8,128)}, s32[]{:T(128)}, s32[]{:T(128)}, /*index=5*/s32[]{:T(128)}, s32[]{:T(128)}) while((s32[]{:T(128)}, f32[3072,768]{1,0:T(8,128)}, f32[3072,768]{1,0:T(8,128)}, s32[]{:T(128)}, s32[]{:T(128)}, /*index=5*/s32[]{:T(128)}, s32[]{:T(128)}) %tuple.56), condition=%wide.region_1.2_spmd, body=%wide.region_0.1_spmd.sunk | while | flops 14505745408 | bytes 23621764 | solution.py:45
  251.8 13.5 %cosine_multiply_fusion.2 = (f32[1536,512]{1,0:T(8,128)S(1)}, f32[1536,512]{1,0:T(8,128)S(1)}) fusion(s32[512]{0:T(512)S(1)} %iota_add_fusion.2, f32[1536]{0:T(1024)S(1)} %get-tuple-element.131, f32[1536]{0:T(1024)S(1)} %get-tuple-element.132), kind=kLoop, calls=%fused_computation.8.clone.1 | loop fusion | flops 8650752 | bytes 6305792 | tf_op jit(solution)/shard_map/while/body/eval_jaxpr/mul | solution.py:18
  265.3 33.4 %fusion.28 = f32[3072,768]{1,0:T(8,128)} fusion(f32[3072,768]{1,0:T(8,128)} %get-tuple-element.143, s32[]{:T(128)S(6)} %select_n.61, f32[3072,768]{1,0:T(8,128)} %get-tuple-element.151, f32[1536,512]{1,0:T(8,128)S(1)} %get-tuple-element.133, f32[1536,512]{1,0:T(8,128)S(1)} %get-tuple-element.134), kind=kOutput, calls=%fused_computation.13.clone.1 | convolution fusion | flops 14497087488 | bytes 17301508 | tf_op jit(solution)/shard_map/while/body/eval_jaxpr/dot_general | solution.py:36
  298.7 13.5 %cosine_multiply_fusion.2 = (f32[1536,512]{1,0:T(8,128)S(1)}, f32[1536,512]{1,0:T(8,128)S(1)}) fusion(s32[512]{0:T(512)S(1)} %iota_add_fusion.2, f32[1536]{0:T(1024)S(1)} %get-tuple-element.131, f32[1536]{0:T(1024)S(1)} %get-tuple-element.132), kind=kLoop, calls=%fused_computation.8.clone.1 | loop fusion | flops 8650752 | bytes 6305792 | tf_op jit(solution)/shard_map/while/body/eval_jaxpr/mul | solution.py:18
  312.2 33.4 %fusion.28 = f32[3072,768]{1,0:T(8,128)} fusion(f32[3072,768]{1,0:T(8,128)} %get-tuple-element.143, s32[]{:T(128)S(6)} %select_n.61, f32[3072,768]{1,0:T(8,128)} %get-tuple-element.151, f32[1536,512]{1,0:T(8,128)S(1)} %get-tuple-element.133, f32[1536,512]{1,0:T(8,128)S(1)} %get-tuple-element.134), kind=kOutput, calls=%fused_computation.13.clone.1 | convolution fusion | flops 14497087488 | bytes 17301508 | tf_op jit(solution)/shard_map/while/body/eval_jaxpr/dot_general | solution.py:36
  345.7 13.5 %cosine_multiply_fusion.2 = (f32[1536,512]{1,0:T(8,128)S(1)}, f32[1536,512]{1,0:T(8,128)S(1)}) fusion(s32[512]{0:T(512)S(1)} %iota_add_fusion.2, f32[1536]{0:T(1024)S(1)} %get-tuple-element.131, f32[1536]{0:T(1024)S(1)} %get-tuple-element.132), kind=kLoop, calls=%fused_computation.8.clone.1 | loop fusion | flops 8650752 | bytes 6305792 | tf_op jit(solution)/shard_map/while/body/eval_jaxpr/mul | solution.py:18
  359.2 33.4 %fusion.28 = f32[3072,768]{1,0:T(8,128)} fusion(f32[3072,768]{1,0:T(8,128)} %get-tuple-element.143, s32[]{:T(128)S(6)} %select_n.61, f32[3072,768]{1,0:T(8,128)} %get-tuple-element.151, f32[1536,512]{1,0:T(8,128)S(1)} %get-tuple-element.133, f32[1536,512]{1,0:T(8,128)S(1)} %get-tuple-element.134), kind=kOutput, calls=%fused_computation.13.clone.1 | convolution fusion | flops 14497087488 | bytes 17301508 | tf_op jit(solution)/shard_map/while/body/eval_jaxpr/dot_general | solution.py:36
  392.6 13.5 %cosine_multiply_fusion.2 = (f32[1536,512]{1,0:T(8,128)S(1)}, f32[1536,512]{1,0:T(8,128)S(1)}) fusion(s32[512]{0:T(512)S(1)} %iota_add_fusion.2, f32[1536]{0:T(1024)S(1)} %get-tuple-element.131, f32[1536]{0:T(1024)S(1)} %get-tuple-element.132), kind=kLoop, calls=%fused_computation.8.clone.1 | loop fusion | flops 8650752 | bytes 6305792 | tf_op jit(solution)/shard_map/while/body/eval_jaxpr/mul | solution.py:18
  406.2 33.4 %fusion.28 = f32[3072,768]{1,0:T(8,128)} fusion(f32[3072,768]{1,0:T(8,128)} %get-tuple-element.143, s32[]{:T(128)S(6)} %select_n.61, f32[3072,768]{1,0:T(8,128)} %get-tuple-element.151, f32[1536,512]{1,0:T(8,128)S(1)} %get-tuple-element.133, f32[1536,512]{1,0:T(8,128)S(1)} %get-tuple-element.134), kind=kOutput, calls=%fused_computation.13.clone.1 | convolution fusion | flops 14497087488 | bytes 17301508 | tf_op jit(solution)/shard_map/while/body/eval_jaxpr/dot_general | solution.py:36
  439.6 13.5 %cosine_multiply_fusion.2 = (f32[1536,512]{1,0:T(8,128)S(1)}, f32[1536,512]{1,0:T(8,128)S(1)}) fusion(s32[512]{0:T(512)S(1)} %iota_add_fusion.2, f32[1536]{0:T(1024)S(1)} %get-tuple-element.131, f32[1536]{0:T(1024)S(1)} %get-tuple-element.132), kind=kLoop, calls=%fused_computation.8.clone.1 | loop fusion | flops 8650752 | bytes 6305792 | tf_op jit(solution)/shard_map/while/body/eval_jaxpr/mul | solution.py:18
  453.1 33.4 %fusion.28 = f32[3072,768]{1,0:T(8,128)} fusion(f32[3072,768]{1,0:T(8,128)} %get-tuple-element.143, s32[]{:T(128)S(6)} %select_n.61, f32[3072,768]{1,0:T(8,128)} %get-tuple-element.151, f32[1536,512]{1,0:T(8,128)S(1)} %get-tuple-element.133, f32[1536,512]{1,0:T(8,128)S(1)} %get-tuple-element.134), kind=kOutput, calls=%fused_computation.13.clone.1 | convolution fusion | flops 14497087488 | bytes 17301508 | tf_op jit(solution)/shard_map/while/body/eval_jaxpr/dot_general | solution.py:36
  486.5 13.5 %cosine_multiply_fusion.2 = (f32[1536,512]{1,0:T(8,128)S(1)}, f32[1536,512]{1,0:T(8,128)S(1)}) fusion(s32[512]{0:T(512)S(1)} %iota_add_fusion.2, f32[1536]{0:T(1024)S(1)} %get-tuple-element.131, f32[1536]{0:T(1024)S(1)} %get-tuple-element.132), kind=kLoop, calls=%fused_computation.8.clone.1 | loop fusion | flops 8650752 | bytes 6305792 | tf_op jit(solution)/shard_map/while/body/eval_jaxpr/mul | solution.py:18
  500.0 33.4 %fusion.28 = f32[3072,768]{1,0:T(8,128)} fusion(f32[3072,768]{1,0:T(8,128)} %get-tuple-element.143, s32[]{:T(128)S(6)} %select_n.61, f32[3072,768]{1,0:T(8,128)} %get-tuple-element.151, f32[1536,512]{1,0:T(8,128)S(1)} %get-tuple-element.133, f32[1536,512]{1,0:T(8,128)S(1)} %get-tuple-element.134), kind=kOutput, calls=%fused_computation.13.clone.1 | convolution fusion | flops 14497087488 | bytes 17301508 | tf_op jit(solution)/shard_map/while/body/eval_jaxpr/dot_general | solution.py:36
  533.4 9.5 %copy.18 = f32[8,384,768]{1,2,0:T(8,128)} copy(f32[8,384,768]{2,1,0:T(8,128)} %bitcast.41) | data formatting | bytes 18874368 | tf_op jit(solution)/shard_map/all_to_all | solution.py:46
  543.0 5.0 all-to-all-start.1
  548.1 9.6 %copy.19 = f32[384,6144]{0,1:T(8,128)} copy(f32[384,6144]{1,0:T(8,128)} %param.7) | data formatting | bytes 18874368 | tf_op args[1]
  557.7 195.0 %all-to-all-done.1 = f32[8,384,768]{1,2,0:T(8,128)} async-done(((f32[8,384,768]{1,2,0:T(8,128)}), f32[8,384,768]{1,2,0:T(8,128)}, u32[]{:S(2)}, u32[]{:S(2)}) %all-to-all-start.1) | async-done | bytes 9437216 | tf_op jit(solution)/shard_map/all_to_all | solution.py:46
  752.7 11.2 %bitcast_multiply_fusion = f32[384,6144]{0,1:T(8,128)} fusion(f32[384,6144]{0,1:T(8,128)} %copy.19, f32[8,384,768]{1,2,0:T(8,128)} %all-to-all-done.1), kind=kLoop, calls=%fused_computation.19 | loop fusion | flops 2359296 | bytes 28311552 | tf_op jit(solution)/shard_map/mul | solution.py:47
  764.0 21.0 %fusion.16 = f32[16,384,128]{2,1,0:T(8,128)} fusion(f32[384,384,16]{0,2,1:T(8,128)} %bitcast.40, f32[384,128]{1,0:T(8,128)S(1)} %copy-done.1), kind=kOutput, calls=%fused_computation.22 | convolution fusion | flops 3623878656 | bytes 12779520 | tf_op jit(solution)/shard_map/xyz,yr->zxr/dot_general | solution.py:51
  785.1 37.0 %reduce-scatter.2.cloned.1.call-done = f32[4,384,128]{2,1,0:T(8,128)} async-done(((f32[16,384,128]{2,1,0:T(8,128)}), f32[4,384,128]{2,1,0:T(8,128)}) %reduce-scatter.2.cloned.1.call-update) | async-done | bytes 786448 | tf_op jit(solution)/shard_map/reduce_scatter | solution.py:50
  826.9 71.6 %all-reduce.3.cloned.1.call-done = f32[4,256,128]{2,0,1:T(4,128)} async-done(((f32[4,256,128]{2,0,1:T(4,128)}), f32[4,256,128]{2,0,1:T(4,128)}) %all-reduce.3.cloned.1.call-update) | async-done | bytes 524304
  (36 shorter events, 29.3 us)
Async XLA Ops:
  7.2 814.9 %copy-start = (f32[384,256]{1,0:T(8,128)S(1)}, f32[384,256]{1,0:T(8,128)}, u32[]{:S(2)}) copy-start(f32[384,256]{1,0:T(8,128)} %param.9) | copy-start | bytes 1179652
  26.4 212.9 %all-to-all-start = ((f32[8,2,192,768]{3,2,1,0:T(8,128)}), f32[8,2,192,768]{3,2,1,0:T(8,128)}, u32[]{:S(2)}, u32[]{:S(2)}) async-start(f32[8,2,192,768]{3,2,1,0:T(8,128)} %bitcast_dynamic-update-slice_fusion), calls=%async_computation | async-start | bytes 18874368 | tf_op jit(solution)/shard_map/all_to_all | solution.py:26
  543.0 209.8 %all-to-all-start.1 = ((f32[8,384,768]{1,2,0:T(8,128)}), f32[8,384,768]{1,2,0:T(8,128)}, u32[]{:S(2)}, u32[]{:S(2)}) async-start(f32[8,384,768]{1,2,0:T(8,128)} %copy.18), calls=%async_computation.1 | async-start | bytes 18874368 | tf_op jit(solution)/shard_map/all_to_all | solution.py:46
  548.0 274.1 %reduce-scatter.2.cloned.1.call-start = ((), (), s32[]{:S(2)}) async-start(), calls=%async_computation.3 | async-start | bytes 3932160 | tf_op jit(solution)/shard_map/reduce_scatter | solution.py:50
  557.7 206.3 %copy-start.1 = (f32[384,128]{1,0:T(8,128)S(1)}, f32[384,128]{1,0:T(8,128)}, u32[]{:S(2)}) copy-start(f32[384,128]{1,0:T(8,128)} %param.8) | copy-start | bytes 589828
  764.0 61.7 %copy-start.2 = (u32[32]{0:T(128)S(1)}, u32[32]{0:T(128)}, u32[]{:S(2)}) copy-start(u32[32]{0:T(128)} %constant.99) | copy-start | bytes 388
  785.0 113.6 %all-reduce.3.cloned.1.call-start = ((), (), s32[]{:S(2)}) async-start(), calls=%async_computation.4 | async-start | bytes 1048576
Sparse Core Ops, SparseCore 0:
  785.1 36.9 reduce-scatter.1
  825.8 72.7 all-reduce.2
